TPU v7x, 32 devices: a whole 2x2x4 slice. The times are simulated.
32 devices in a mesh: section: 8 (over y, x, core), fsdp: 4 (over z).
Axes of the slice: x: 2, y: 2, z: 4, core: 2. Of those that a mesh axis runs over, the one named last changes fastest.
Arguments:
- layer_input: bfloat16 [8, 512, 4096], P('section', 'fsdp'), may hold values from -6 to 6
- next_cot: bfloat16 [8, 512, 512], P('section', 'fsdp'), may hold values from -6 to 6
- w_value: bfloat16 [8, 4096, 512], P('section', 'fsdp'), may hold values from -0.25 to 0.25
- micro_ids: int32 [8, 4], P('section', 'fsdp'), may hold values from 0 to 1
Outputs:
- grad_input: bfloat16 [8, 512, 4096], P('section', 'fsdp')
- grad_sum: float32 [8, 4096, 512], P('section', 'fsdp')
- grad_square: float32 [8, 4096, 512], P('section', 'fsdp')
All inputs are finite; a program needn't handle non-finite values.
Results may differ from a plain program's by a relative error of at most 0.0037.
Values may be sent and summed in bfloat16 or wider, within the bound.
A program may use at most 64 MiB of HBM per device.

v0:
```python
import functools

import jax
import jax.numpy as jnp
from jax import lax
from jax.experimental import pallas as pl
from jax.experimental.pallas import tpu as pltpu
from jax.sharding import PartitionSpec as P

MICRO = 2
MESH = pl.DeviceIdType.MESH


def kernel(
    n, ns, li, cot, w, mid, gi, gs, gq,
    inc, lix, gis, ids, wv,
    perm_s, perm_r, right_s, left_s, cot_r, li_s, li_r, gi_s, gi_r, id_s, id_r, own_s,
):
    f = lax.axis_index("fsdp")
    s = lax.axis_index("section")
    behind = lax.rem(s + ns - 1, ns)
    ahead = lax.rem(s + 1, ns)
    tokens, share = lix.shape[1], lix.shape[2]
    columns = inc.shape[2]

    def share_of(ref, part, rows=slice(None)):
        return ref.at[rows, pl.ds(pl.multiple_of(part * share, share), share)]

    def li_copy(target, rows=slice(None)):
        return pltpu.make_async_remote_copy(
            src_ref=share_of(li, target, rows),
            dst_ref=lix.at[f, rows],
            send_sem=li_s.at[target],
            recv_sem=li_r.at[f],
            device_id={"fsdp": target},
            device_id_type=MESH,
        )

    def cot_copy(block, target, sem):
        return pltpu.make_async_remote_copy(
            src_ref=inc.at[block],
            dst_ref=inc.at[block],
            send_sem=sem.at[block],
            recv_sem=cot_r.at[block],
            device_id={"fsdp": target},
            device_id_type=MESH,
        )

    def gi_copy(target):
        return pltpu.make_async_remote_copy(
            src_ref=gis.at[target],
            dst_ref=share_of(gi, f),
            send_sem=gi_s.at[target],
            recv_sem=gi_r.at[f],
            device_id={"fsdp": target},
            device_id_type=MESH,
        )

    def id_copy(target):
        return pltpu.make_async_remote_copy(
            src_ref=ids.at[f],
            dst_ref=ids.at[f],
            send_sem=id_s.at[target],
            recv_sem=id_r.at[f],
            device_id={"fsdp": target},
            device_id_type=MESH,
        )

    barrier = pltpu.get_barrier_semaphore()
    pl.semaphore_signal(barrier, inc=1, device_id={"section": ahead}, device_id_type=MESH)
    for step in range(1, n):
        pl.semaphore_signal(
            barrier, inc=1, device_id={"fsdp": lax.rem(f + step, n)}, device_id_type=MESH
        )
    pl.semaphore_wait(barrier, n)

    permute = pltpu.make_async_remote_copy(
        src_ref=cot,
        dst_ref=inc.at[f],
        send_sem=perm_s,
        recv_sem=perm_r,
        device_id={"section": behind},
        device_id_type=MESH,
    )

    pieces = min(n, 4)
    rows = tokens // pieces

    def li_piece(piece):
        if piece >= pieces:
            return
        window = pl.ds(piece * rows, rows)

        @pl.when(f < n - 1)
        def _():
            li_copy(n - 1, window).start()

        @pl.when(f > 0)
        def _():
            li_copy(0, window).start()

    def forward(step):
        @pl.when((f - step >= 0) & (f < n - 1))
        def _():
            cot_copy(f - step, f + 1, right_s).start()

        @pl.when((f + step < n) & (f > 0))
        def _():
            cot_copy(f + step, f - 1, left_s).start()

    def arrived(step):
        @pl.when(f - step >= 0)
        def _():
            cot_copy(f - step, f, right_s).wait_recv()

        @pl.when(f + step < n)
        def _():
            cot_copy(f + step, f, left_s).wait_recv()

    li_piece(0)
    permute.start()
    weights = pltpu.make_async_copy(w, wv, own_s.at[0])
    weights.start()
    own_li = pltpu.make_async_copy(share_of(li, f), lix.at[f], own_s.at[1])
    own_li.start()
    ids[f] = jnp.full(ids.shape[1:], mid[0, 0], jnp.int32)
    permute.wait_recv()
    forward(0)
    for step in range(1, n):
        id_copy(lax.rem(f + step, n)).start()
    li_piece(1)
    for step in range(1, n - 1):
        arrived(step)
        forward(step)
        li_piece(step + 1)
    for piece in range(n, pieces):
        li_piece(piece)
    for turn in range(1, n - 1):
        @pl.when(n - 1 - turn > f)
        def _():
            li_copy(n - 1 - turn).start()

        @pl.when(turn < f)
        def _():
            li_copy(turn).start()
    arrived(n - 1)

    weights.wait()

    def input_block(block, carry):
        gis[block] = lax.dot_general(
            inc[block], wv[...], (((1,), (1,)), ((), ())), preferred_element_type=jnp.float32
        ).astype(gis.dtype)
        return carry

    lax.fori_loop(0, n, input_block, 0)
    own_gi = pltpu.make_async_copy(gis.at[f], share_of(gi, f), own_s.at[2])
    own_gi.start()
    for turn in range(n - 1):
        @pl.when(n - 1 - turn > f)
        def _():
            gi_copy(n - 1 - turn).start()

        @pl.when(turn < f)
        def _():
            gi_copy(turn).start()

    own_li.wait()

    def others(action):
        def run(step, carry):
            action(lax.rem(f + step, n))
            return carry

        lax.fori_loop(1, n, run, 0)

    def li_wait(peer):
        pltpu.make_async_remote_copy(
            src_ref=share_of(li, peer),
            dst_ref=lix.at[peer],
            send_sem=li_s.at[peer],
            recv_sem=li_r.at[peer],
            device_id={"fsdp": peer},
            device_id_type=MESH,
        ).wait()
        pltpu.make_async_remote_copy(
            src_ref=ids.at[f],
            dst_ref=ids.at[peer],
            send_sem=id_s.at[peer],
            recv_sem=id_r.at[peer],
            device_id={"fsdp": peer},
            device_id_type=MESH,
        ).wait()

    others(li_wait)

    inverse = 1.0 / tokens
    tile = 128

    def weight_rows(index, carry):
        start = pl.multiple_of(index * tile, tile)
        micro = [jnp.zeros((tile, columns), jnp.float32) for _ in range(MICRO)]
        for block in range(n):
            product = lax.dot_general(
                lix[block, :, pl.ds(start, tile)],
                inc[block],
                (((0,), (0,)), ((), ())),
                preferred_element_type=jnp.float32,
            )
            product = (product * inverse).astype(jnp.bfloat16).astype(jnp.float32)
            owner = jnp.broadcast_to(ids[block][:1, :1], product.shape)
            for m in range(MICRO):
                micro[m] = micro[m] + jnp.where(owner == m, product, 0.0)
        total = micro[0]
        square = micro[0] * micro[0]
        for m in range(1, MICRO):
            total = total + micro[m]
            square = square + micro[m] * micro[m]
        gs[pl.ds(start, tile), :] = total
        gq[pl.ds(start, tile), :] = square
        return carry

    lax.fori_loop(0, share // tile, weight_rows, 0)

    own_gi.wait()
    permute.wait_send()
    for step in range(n - 1):
        @pl.when((f - step >= 0) & (f < n - 1))
        def _():
            cot_copy(f - step, f + 1, right_s).wait_send()

        @pl.when((f + step < n) & (f > 0))
        def _():
            cot_copy(f + step, f - 1, left_s).wait_send()

    def gi_wait(peer):
        pltpu.make_async_remote_copy(
            src_ref=gis.at[peer],
            dst_ref=share_of(gi, peer),
            send_sem=gi_s.at[peer],
            recv_sem=gi_r.at[peer],
            device_id={"fsdp": peer},
            device_id_type=MESH,
        ).wait()

    others(gi_wait)


def settle_kernel(cuts, *refs):
    count = len(refs) // 2
    sems = refs[-1]
    copies = []
    for index in range(count):
        source, target = refs[index], refs[count + index]
        rows = source.shape[0] // cuts
        for cut in range(cuts):
            window = pl.ds(cut * rows, rows)
            copies.append(
                pltpu.make_async_copy(source.at[window], target.at[window], sems.at[index, cut])
            )
    for copy in copies:
        copy.start()
    for copy in copies:
        copy.wait()


def settle(*arrays):
    cuts = 1
    return pl.pallas_call(
        functools.partial(settle_kernel, cuts),
        out_shape=tuple(jax.ShapeDtypeStruct(a.shape, a.dtype) for a in arrays),
        in_specs=[pl.BlockSpec(memory_space=pl.ANY)] * len(arrays),
        out_specs=tuple(pl.BlockSpec(memory_space=pltpu.HBM) for _ in arrays),
        scratch_shapes=[pltpu.SemaphoreType.DMA((len(arrays), cuts))],
        compiler_params=pltpu.CompilerParams(vmem_limit_bytes=4 * 2**20),
    )(*[pltpu.with_memory_space_constraint(a, pltpu.VMEM) for a in arrays])


def body(layer_input, next_cot, w_value, micro_ids):
    n = lax.axis_size("fsdp")
    ns = lax.axis_size("section")
    tokens, width = layer_input.shape[1:]
    share, columns = w_value.shape[1:]
    anywhere = pl.BlockSpec(memory_space=pltpu.HBM)
    dma = pltpu.SemaphoreType.DMA
    stay = functools.partial(pltpu.with_memory_space_constraint, memory_space=pltpu.HBM)
    arrays = pl.pallas_call(
        functools.partial(kernel, n, ns),
        out_shape=(
            jax.ShapeDtypeStruct((tokens, width), jnp.bfloat16),
            jax.ShapeDtypeStruct((share, columns), jnp.float32),
            jax.ShapeDtypeStruct((share, columns), jnp.float32),
        ),
        in_specs=[anywhere, anywhere, anywhere, pl.BlockSpec(memory_space=pltpu.SMEM)],
        out_specs=OUT_SPECS,
        scratch_shapes=[
            pltpu.VMEM((n, tokens, columns), jnp.bfloat16),
            pltpu.VMEM((n, tokens, share), jnp.bfloat16),
            pltpu.VMEM((n, tokens, share), jnp.bfloat16),
            pltpu.VMEM((n, 8, 128), jnp.int32),
            pltpu.VMEM((share, columns), jnp.bfloat16),
            dma, dma, dma((n,)), dma((n,)), dma((n,)), dma((n,)), dma((n,)),
            dma((n,)), dma((n,)), dma((n,)), dma((n,)), dma((3,)),
        ],
        compiler_params=pltpu.CompilerParams(
            collective_id=0, has_side_effects=True, vmem_limit_bytes=40 * 2**20
        ),
    )(stay(layer_input[0]), stay(next_cot[0]), stay(w_value[0]), micro_ids)
    grad_input, grad_sum, grad_square = settle(*arrays)
    return (grad_input[None], grad_sum[None], grad_square[None])


OUT_SPECS = (
    pl.BlockSpec(memory_space=pl.ANY),
    pl.BlockSpec(memory_space=pltpu.VMEM),
    pl.BlockSpec(memory_space=pltpu.VMEM),
)


def solution(mesh):
    spec = P("section", "fsdp", None)
    return jax.shard_map(
        body,
        mesh=mesh,
        in_specs=(spec, spec, spec, P("section", "fsdp")),
        out_specs=(spec, spec, spec),
        check_vma=False,
    )
```

profile of v0, /device:TPU:13, one launch (start us, length us, event | category | flops | bytes accessed | tf_op | source)
XLA Modules:
  0.0 58.9 jit_solution(255376371317480943)
XLA Ops:
  1.3 55.2 %shard_map.67 = (bf16[128,4096]{1,0:T(8,128)(2,1)S(1)}, f32[1024,512]{1,0:T(8,128)S(1)}, f32[1024,512]{1,0:T(8,128)S(1)}) custom-call(bf16[128,4096]{1,0:T(8,128)(2,1)} %bitcast.6, bf16[128,512]{1,0:T(8,128)(2,1)} %bitcast.8, bf16[1024,512]{1,0:T(8,128)(2,1)} %bitcast.7, s32[1,1]{1,0:T(1,128)S(6)} %copy.7.mid), custom_call_target="tpu_custom_call" | custom-call | tf_op jit(solution)/shard_map/pallas_call | solution.py:287
  56.5 2.4 %shard_map.68 = (bf16[128,4096]{1,0:T(8,128)(2,1)}, f32[1024,512]{1,0:T(8,128)}, f32[1024,512]{1,0:T(8,128)}) custom-call(bf16[128,4096]{1,0:T(8,128)(2,1)S(1)} %get-tuple-element.9.refs_0_, f32[1024,512]{1,0:T(8,128)S(1)} %get-tuple-element.10.refs_1_, f32[1024,512]{1,0:T(8,128)S(1)} %get-tuple-element.11.refs_2_), custom_call_target="tpu_custom_call" | custom-call | tf_op jit(solution)/shard_map/pallas_call | solution.py:269
where the time goes:
time: 59.5 us; the launch traced here: 58.9 us
  Pallas kernels  57.6 us (97%)
  between operations  1.29 us (2%)
    pallas_call x1, Pallas kernels, body(): pl.pallas_call(functools.partial(kernel, n, ns), out_shape=(jax.ShapeDtyp...  55.2 us
    pallas_call x1, Pallas kernels, settle(): pl.pallas_call(functools.partial(settle_kernel, cuts), out_shape=tuple((j...  2.38 us

commit v1 on v0

--- a/solution.py
+++ b/solution.py
@@ -9,12 +9,17 @@
 
 MICRO = 2
 MESH = pl.DeviceIdType.MESH
+PIECES = 4
+HEAD = 3
+FAR = 1
+BETWEEN = 2
 
 
 def kernel(
     n, ns, li, cot, w, mid, gi, gs, gq,
     inc, lix, gis, ids, wv,
     perm_s, perm_r, right_s, left_s, cot_r, li_s, li_r, gi_s, gi_r, id_s, id_r, own_s,
+    above, below,
 ):
     f = lax.axis_index("fsdp")
     s = lax.axis_index("section")
@@ -56,23 +61,15 @@
             device_id_type=MESH,
         )
 
-    def id_copy(target):
+    def id_copy(target, owner):
         return pltpu.make_async_remote_copy(
-            src_ref=ids.at[f],
-            dst_ref=ids.at[f],
+            src_ref=ids.at[owner],
+            dst_ref=ids.at[owner],
             send_sem=id_s.at[target],
-            recv_sem=id_r.at[f],
+            recv_sem=id_r.at[owner],
             device_id={"fsdp": target},
             device_id_type=MESH,
         )
-
-    barrier = pltpu.get_barrier_semaphore()
-    pl.semaphore_signal(barrier, inc=1, device_id={"section": ahead}, device_id_type=MESH)
-    for step in range(1, n):
-        pl.semaphore_signal(
-            barrier, inc=1, device_id={"fsdp": lax.rem(f + step, n)}, device_id_type=MESH
-        )
-    pl.semaphore_wait(barrier, n)
 
     permute = pltpu.make_async_remote_copy(
         src_ref=cot,
@@ -82,22 +79,38 @@
         device_id={"section": behind},
         device_id_type=MESH,
     )
-
-    pieces = min(n, 4)
+    weights = pltpu.make_async_copy(w, wv, own_s.at[0])
+    own_li = pltpu.make_async_copy(share_of(li, f), lix.at[f], own_s.at[1])
+
+    def tell(sem, target, cond):
+        @pl.when(cond)
+        def _():
+            pl.semaphore_signal(sem, inc=1, device_id={"fsdp": target}, device_id_type=MESH)
+
+    barrier = pltpu.get_barrier_semaphore()
+    tell(barrier, f + 1, f < n - 1)
+    pl.semaphore_signal(barrier, inc=1, device_id={"section": ahead}, device_id_type=MESH)
+    pl.semaphore_wait(barrier, 1 + (f > 0).astype(jnp.int32))
+
+    pieces = PIECES
     rows = tokens // pieces
 
-    def li_piece(piece):
-        if piece >= pieces:
-            return
+    half = n // 2
+    head = min(HEAD, pieces)
+    total = half * pieces
+
+    def crossing(index):
+        owner, piece = index // pieces, index % pieces
         window = pl.ds(piece * rows, rows)
-
-        @pl.when(f < n - 1)
-        def _():
-            li_copy(n - 1, window).start()
-
-        @pl.when(f > 0)
-        def _():
-            li_copy(0, window).start()
+        first = owner == half - 1 and piece < head
+
+        @pl.when((f < half - 1) if first else (f < half))
+        def _():
+            li_copy(n - 1 - owner, window).start()
+
+        @pl.when((f > half) if first else (f >= half))
+        def _():
+            li_copy(owner, window).start()
 
     def forward(step):
         @pl.when((f - step >= 0) & (f < n - 1))
@@ -117,53 +130,91 @@
         def _():
             cot_copy(f + step, f, left_s).wait_recv()
 
-    li_piece(0)
+    tell(above.at[1], f - 1, f > 0)
     permute.start()
-    weights = pltpu.make_async_copy(w, wv, own_s.at[0])
+
+    @pl.when(f == half)
+    def _():
+        li_copy(half - 1, pl.ds(0, head * rows)).start()
+
+    @pl.when(f < n - 1)
+    def _():
+        pl.semaphore_wait(above.at[1], 1)
+
+    @pl.when(f == half - 1)
+    def _():
+        li_copy(half, pl.ds(0, head * rows)).start()
+
+    if n > 2:
+        tell(above.at[2], f - 1, (f > 0) & (f + 1 < n))
+        tell(below.at[2], f + 1, (f < n - 1) & (f - 1 >= 0))
     weights.start()
-    own_li = pltpu.make_async_copy(share_of(li, f), lix.at[f], own_s.at[1])
     own_li.start()
     ids[f] = jnp.full(ids.shape[1:], mid[0, 0], jnp.int32)
+    for d in range(2, n):
+        @pl.when(f + d < n)
+        def _():
+            pl.semaphore_wait(above.at[d], 1)
+
+        @pl.when(f - d >= 0)
+        def _():
+            pl.semaphore_wait(below.at[d], 1)
+
+        if d + 1 < n:
+            tell(above.at[d + 1], f - 1, (f > 0) & (f + d < n))
+            tell(below.at[d + 1], f + 1, (f < n - 1) & (f - d >= 0))
+
+    issued = 0
+    for index in range(issued, FAR):
+        crossing(index)
+    issued = FAR
     permute.wait_recv()
     forward(0)
     for step in range(1, n):
-        id_copy(lax.rem(f + step, n)).start()
-    li_piece(1)
+        target = lax.rem(f + step, n)
+        id_copy(target, f).start()
     for step in range(1, n - 1):
+        upto = min(total, issued + BETWEEN)
+        for index in range(issued, upto):
+            crossing(index)
+        issued = upto
         arrived(step)
         forward(step)
-        li_piece(step + 1)
-    for piece in range(n, pieces):
-        li_piece(piece)
-    for turn in range(1, n - 1):
-        @pl.when(n - 1 - turn > f)
-        def _():
-            li_copy(n - 1 - turn).start()
-
-        @pl.when(turn < f)
-        def _():
-            li_copy(turn).start()
-    arrived(n - 1)
+    for index in range(issued, total):
+        crossing(index)
+    for distance in range(n - 1, 0, -1):
+        @pl.when((f + distance < n) & ((f + distance < half) | (f >= half)))
+        def _():
+            li_copy(f + distance).start()
+
+        @pl.when((f - distance >= 0) & ((f < half) | (f - distance >= half)))
+        def _():
+            li_copy(f - distance).start()
 
     weights.wait()
 
-    def input_block(block, carry):
+    def input_block(block):
         gis[block] = lax.dot_general(
             inc[block], wv[...], (((1,), (1,)), ((), ())), preferred_element_type=jnp.float32
         ).astype(gis.dtype)
+
+    arrived(n - 1)
+
+    def input_blocks(block, carry):
+        input_block(block)
         return carry
 
-    lax.fori_loop(0, n, input_block, 0)
+    lax.fori_loop(0, n, input_blocks, 0)
     own_gi = pltpu.make_async_copy(gis.at[f], share_of(gi, f), own_s.at[2])
     own_gi.start()
-    for turn in range(n - 1):
-        @pl.when(n - 1 - turn > f)
-        def _():
-            gi_copy(n - 1 - turn).start()
-
-        @pl.when(turn < f)
-        def _():
-            gi_copy(turn).start()
+    for d in range(n - 1, 0, -1):
+        @pl.when(f + d < n)
+        def _():
+            gi_copy(f + d).start()
+
+        @pl.when(f - d >= 0)
+        def _():
+            gi_copy(f - d).start()
 
     own_li.wait()
 
@@ -183,14 +234,7 @@
             device_id={"fsdp": peer},
             device_id_type=MESH,
         ).wait()
-        pltpu.make_async_remote_copy(
-            src_ref=ids.at[f],
-            dst_ref=ids.at[peer],
-            send_sem=id_s.at[peer],
-            recv_sem=id_r.at[peer],
-            device_id={"fsdp": peer},
-            device_id_type=MESH,
-        ).wait()
+        id_copy(peer, peer).wait()
 
     others(li_wait)
 
@@ -301,6 +345,7 @@
             pltpu.VMEM((share, columns), jnp.bfloat16),
             dma, dma, dma((n,)), dma((n,)), dma((n,)), dma((n,)), dma((n,)),
             dma((n,)), dma((n,)), dma((n,)), dma((n,)), dma((3,)),
+            pltpu.SemaphoreType.REGULAR((n,)), pltpu.SemaphoreType.REGULAR((n,)),
         ],
         compiler_params=pltpu.CompilerParams(
             collective_id=0, has_side_effects=True, vmem_limit_bytes=40 * 2**20

time: 59.5 us -> 59.8 us (level)
  the two profiles are of different devices: /device:TPU:13 before, /device:TPU:16 now
where the time goes in v1:
time: 59.8 us; the launch traced here: 59.6 us
  Pallas kernels  58.4 us (98%)
  between operations  1.29 us (2%)
    pallas_call x1, Pallas kernels, body(): pl.pallas_call(functools.partial(kernel, n, ns), out_shape=(jax.ShapeDtyp...  56 us
    pallas_call x1, Pallas kernels, settle(): pl.pallas_call(functools.partial(settle_kernel, cuts), out_shape=tuple((j...  2.38 us

profile of v1, /device:TPU:16, one launch (start us, length us, event | category | flops | bytes accessed | tf_op | source)
XLA Modules:
  0.0 59.6 jit_solution(14687672393681881782)
XLA Ops:
  1.3 56.0 %shard_map.67 = (bf16[128,4096]{1,0:T(8,128)(2,1)S(1)}, f32[1024,512]{1,0:T(8,128)S(1)}, f32[1024,512]{1,0:T(8,128)S(1)}) custom-call(bf16[128,4096]{1,0:T(8,128)(2,1)} %bitcast.6, bf16[128,512]{1,0:T(8,128)(2,1)} %bitcast.8, bf16[1024,512]{1,0:T(8,128)(2,1)} %bitcast.7, s32[1,1]{1,0:T(1,128)S(6)} %copy.7.mid), custom_call_target="tpu_custom_call" | custom-call | tf_op jit(solution)/shard_map/pallas_call | solution.py:331
  57.3 2.4 %shard_map.68 = (bf16[128,4096]{1,0:T(8,128)(2,1)}, f32[1024,512]{1,0:T(8,128)}, f32[1024,512]{1,0:T(8,128)}) custom-call(bf16[128,4096]{1,0:T(8,128)(2,1)S(1)} %get-tuple-element.9.refs_0_, f32[1024,512]{1,0:T(8,128)S(1)} %get-tuple-element.10.refs_1_, f32[1024,512]{1,0:T(8,128)S(1)} %get-tuple-element.11.refs_2_), custom_call_target="tpu_custom_call" | custom-call | tf_op jit(solution)/shard_map/pallas_call | solution.py:313

commit v2 on v1

--- a/solution.py
+++ b/solution.py
@@ -11,7 +11,7 @@
 MESH = pl.DeviceIdType.MESH
 PIECES = 4
 HEAD = 3
-FAR = 1
+FAR = 0
 BETWEEN = 2
 
 
@@ -19,7 +19,7 @@
     n, ns, li, cot, w, mid, gi, gs, gq,
     inc, lix, gis, ids, wv,
     perm_s, perm_r, right_s, left_s, cot_r, li_s, li_r, gi_s, gi_r, id_s, id_r, own_s,
-    above, below,
+    above, below, pair,
 ):
     f = lax.axis_index("fsdp")
     s = lax.axis_index("section")
@@ -89,8 +89,24 @@
 
     barrier = pltpu.get_barrier_semaphore()
     tell(barrier, f + 1, f < n - 1)
-    pl.semaphore_signal(barrier, inc=1, device_id={"section": ahead}, device_id_type=MESH)
-    pl.semaphore_wait(barrier, 1 + (f > 0).astype(jnp.int32))
+
+    @pl.when(s < ns - 1)
+    def _():
+        pl.semaphore_signal(barrier, inc=1, device_id={"section": ahead}, device_id_type=MESH)
+
+    @pl.when(s == 0)
+    def _():
+        pl.semaphore_signal(barrier, inc=1, device_id={"section": behind}, device_id_type=MESH)
+
+    greetings = (f > 0).astype(jnp.int32) + (s > 0).astype(jnp.int32) + (s == ns - 1).astype(jnp.int32)
+
+    @pl.when(greetings > 0)
+    def _():
+        pl.semaphore_wait(barrier, greetings)
+
+    @pl.when(s == ns - 1)
+    def _():
+        pl.semaphore_signal(pair, inc=1, device_id={"section": ahead}, device_id_type=MESH)
 
     pieces = PIECES
     rows = tokens // pieces
@@ -131,7 +147,10 @@
             cot_copy(f + step, f, left_s).wait_recv()
 
     tell(above.at[1], f - 1, f > 0)
-    permute.start()
+
+    @pl.when(s > 0)
+    def _():
+        permute.start()
 
     @pl.when(f == half)
     def _():
@@ -164,10 +183,14 @@
             tell(above.at[d + 1], f - 1, (f > 0) & (f + d < n))
             tell(below.at[d + 1], f + 1, (f < n - 1) & (f - d >= 0))
 
-    issued = 0
-    for index in range(issued, FAR):
+    @pl.when(s == 0)
+    def _():
+        pl.semaphore_wait(pair, 1)
+        permute.start()
+
+    issued = FAR
+    for index in range(issued):
         crossing(index)
-    issued = FAR
     permute.wait_recv()
     forward(0)
     for step in range(1, n):
@@ -345,7 +368,7 @@
             pltpu.VMEM((share, columns), jnp.bfloat16),
             dma, dma, dma((n,)), dma((n,)), dma((n,)), dma((n,)), dma((n,)),
             dma((n,)), dma((n,)), dma((n,)), dma((n,)), dma((3,)),
-            pltpu.SemaphoreType.REGULAR((n,)), pltpu.SemaphoreType.REGULAR((n,)),
+            pltpu.SemaphoreType.REGULAR((n,)), pltpu.SemaphoreType.REGULAR((n,)), pltpu.SemaphoreType.REGULAR,
         ],
         compiler_params=pltpu.CompilerParams(
             collective_id=0, has_side_effects=True, vmem_limit_bytes=40 * 2**20

time: 59.8 us -> 58.7 us (0.982)
  the two profiles are of different devices: /device:TPU:16 before, /device:TPU:13 now
where the time goes in v2:
time: 58.7 us; the launch traced here: 57.6 us
  Pallas kernels  56.3 us (96%)
  between operations  1.29 us (2%)
    pallas_call x1, Pallas kernels, body(): pl.pallas_call(functools.partial(kernel, n, ns), out_shape=(jax.ShapeDtyp...  54 us
    pallas_call x1, Pallas kernels, settle(): pl.pallas_call(functools.partial(settle_kernel, cuts), out_shape=tuple((j...  2.38 us

profile of v2, /device:TPU:13, one launch (start us, length us, event | category | flops | bytes accessed | tf_op | source)
XLA Modules:
  0.0 57.6 jit_solution(16407673954873681875)
XLA Ops:
  1.3 54.0 %shard_map.67 = (bf16[128,4096]{1,0:T(8,128)(2,1)S(1)}, f32[1024,512]{1,0:T(8,128)S(1)}, f32[1024,512]{1,0:T(8,128)S(1)}) custom-call(bf16[128,4096]{1,0:T(8,128)(2,1)} %bitcast.6, bf16[128,512]{1,0:T(8,128)(2,1)} %bitcast.8, bf16[1024,512]{1,0:T(8,128)(2,1)} %bitcast.7, s32[1,1]{1,0:T(1,128)S(6)} %copy.7.mid), custom_call_target="tpu_custom_call" | custom-call | tf_op jit(solution)/shard_map/pallas_call | solution.py:354
  55.2 2.4 %shard_map.68 = (bf16[128,4096]{1,0:T(8,128)(2,1)}, f32[1024,512]{1,0:T(8,128)}, f32[1024,512]{1,0:T(8,128)}) custom-call(bf16[128,4096]{1,0:T(8,128)(2,1)S(1)} %get-tuple-element.9.refs_0_, f32[1024,512]{1,0:T(8,128)S(1)} %get-tuple-element.10.refs_1_, f32[1024,512]{1,0:T(8,128)S(1)} %get-tuple-element.11.refs_2_), custom_call_target="tpu_custom_call" | custom-call | tf_op jit(solution)/shard_map/pallas_call | solution.py:336

commit v3 on v2

v3 whole, which is shorter than its diff:
```python
import functools

import jax
import jax.numpy as jnp
from jax import lax
from jax.experimental import pallas as pl
from jax.experimental.pallas import tpu as pltpu
from jax.sharding import PartitionSpec as P

MICRO = 2
MESH = pl.DeviceIdType.MESH
PIECES = 4
HEAD = (3, 2, 2, 3)
BETWEEN = (2, 1, 2, 2)
TILE = 256
AT_ONCE = 1
INNER = 4


def tell(sem, target, cond):
    @pl.when(cond)
    def _():
        pl.semaphore_signal(sem, inc=1, device_id={"fsdp": target}, device_id_type=MESH)


def share_of(ref, part, share, rows=slice(None)):
    return ref.at[rows, pl.ds(pl.multiple_of(part * share, share), share)]


def gi_copy(peer, owner, gis, gi, gi_s, gi_r, rows=slice(None)):
    return pltpu.make_async_remote_copy(
        src_ref=gis.at[peer, rows],
        dst_ref=share_of(gi, owner, gis.shape[2], rows),
        send_sem=gi_s.at[peer],
        recv_sem=gi_r.at[owner],
        device_id={"fsdp": peer},
        device_id_type=MESH,
    )


def gi_send(n, f, gis, gi, gi_s, gi_r, own_s):
    for d in range(n - 1, 0, -1):
        @pl.when(f + d < n)
        def _():
            gi_copy(f + d, f, gis, gi, gi_s, gi_r).start()

        @pl.when(f - d >= 0)
        def _():
            gi_copy(f - d, f, gis, gi, gi_s, gi_r).start()

    pltpu.make_async_copy(gis.at[f], share_of(gi, f, gis.shape[2]), own_s).start()


def gi_wait(n, f, gis, gi, gi_s, gi_r, own_s):
    pltpu.make_async_copy(gis.at[f], share_of(gi, f, gis.shape[2]), own_s).wait()

    def run(step, carry):
        peer = lax.rem(f + step, n)
        gi_copy(peer, peer, gis, gi, gi_s, gi_r).wait()
        return carry

    lax.fori_loop(1, n, run, 0)


def kernel(
    n, ns, li, cot, w, mid, gi, gis, inc, lix, ids, wv,
    perm_s, perm_r, right_s, left_s, cot_r, li_s, li_r, gi_s, gi_r, id_s, id_r, own_s,
    above, below, pair,
):
    f = lax.axis_index("fsdp")
    s = lax.axis_index("section")
    behind = lax.rem(s + ns - 1, ns)
    ahead = lax.rem(s + 1, ns)
    at_once = lax.rem(s, 2) == AT_ONCE
    early_ahead = lax.rem(ahead, 4) != 0
    turns = (
        jnp.logical_not(at_once),
        at_once & early_ahead,
        at_once & jnp.logical_not(early_ahead) & (s < ns - 1),
        at_once & jnp.logical_not(early_ahead) & (s == ns - 1),
    )
    tokens, share = lix.shape[1], lix.shape[2]
    columns = inc.shape[2]

    def li_copy(target, rows=slice(None)):
        return pltpu.make_async_remote_copy(
            src_ref=share_of(li, target, share, rows),
            dst_ref=lix.at[f, rows],
            send_sem=li_s.at[target],
            recv_sem=li_r.at[f],
            device_id={"fsdp": target},
            device_id_type=MESH,
        )

    def cot_copy(block, target, sem):
        return pltpu.make_async_remote_copy(
            src_ref=inc.at[block],
            dst_ref=inc.at[block],
            send_sem=sem.at[block],
            recv_sem=cot_r.at[block],
            device_id={"fsdp": target},
            device_id_type=MESH,
        )

    def id_copy(target, owner):
        return pltpu.make_async_remote_copy(
            src_ref=ids.at[owner],
            dst_ref=ids.at[owner],
            send_sem=id_s.at[target],
            recv_sem=id_r.at[owner],
            device_id={"fsdp": target},
            device_id_type=MESH,
        )

    permute = pltpu.make_async_remote_copy(
        src_ref=cot,
        dst_ref=inc.at[f],
        send_sem=perm_s,
        recv_sem=perm_r,
        device_id={"section": behind},
        device_id_type=MESH,
    )
    weights = pltpu.make_async_copy(w, wv, own_s.at[0])
    own_li = pltpu.make_async_copy(share_of(li, f, share), lix.at[f], own_s.at[1])

    late, late_ahead = lax.rem(s, 4) == 0, lax.rem(ahead, 4) == 0
    barrier = pltpu.get_barrier_semaphore()
    tell(barrier, f + 1, f < n - 1)

    @pl.when(jnp.logical_not(late_ahead))
    def _():
        pl.semaphore_signal(barrier, inc=1, device_id={"section": ahead}, device_id_type=MESH)

    @pl.when(late)
    def _():
        pl.semaphore_signal(barrier, inc=1, device_id={"section": behind}, device_id_type=MESH)

    greetings = (f > 0).astype(jnp.int32) + 1 - late.astype(jnp.int32) + late_ahead.astype(jnp.int32)

    @pl.when(greetings > 0)
    def _():
        pl.semaphore_wait(barrier, greetings)

    @pl.when(late_ahead)
    def _():
        pl.semaphore_signal(pair, inc=1, device_id={"section": ahead}, device_id_type=MESH)

    pieces = PIECES
    rows = tokens // pieces

    half = n // 2
    total = half * pieces

    def head_rows(turn):
        return min(HEAD[turn], pieces) * rows

    def by_turn(action):
        for turn, condition in enumerate(turns):
            pl.when(condition)(functools.partial(action, turn))

    def crossing(index, turn):
        owner, piece = index // pieces, index % pieces
        window = pl.ds(piece * rows, rows)
        done = owner == half - 1 and piece * rows < head_rows(turn)

        @pl.when((f < half - 1) if done else (f < half))
        def _():
            li_copy(n - 1 - owner, window).start()

        @pl.when((f > half) if done else (f >= half))
        def _():
            li_copy(owner, window).start()

    def near(piece):
        if piece >= pieces:
            return
        window = pl.ds(piece * rows, rows)

        @pl.when((f > 0) & (f < half))
        def _():
            li_copy(0, window).start()

        @pl.when((f >= half) & (f < n - 1))
        def _():
            li_copy(n - 1, window).start()

    def inner():
        for distance in range(n - 1, 0, -1):
            @pl.when(f + distance < half)
            def _():
                li_copy(f + distance).start()

            @pl.when(f - distance >= half)
            def _():
                li_copy(f - distance).start()

    def forward(step):
        @pl.when((f - step >= 0) & (f < n - 1))
        def _():
            cot_copy(f - step, f + 1, right_s).start()

        @pl.when((f + step < n) & (f > 0))
        def _():
            cot_copy(f + step, f - 1, left_s).start()

    def arrived(step):
        @pl.when(f - step >= 0)
        def _():
            cot_copy(f - step, f, right_s).wait_recv()

        @pl.when(f + step < n)
        def _():
            cot_copy(f + step, f, left_s).wait_recv()

    tell(above.at[1], f - 1, f > 0)

    @pl.when(jnp.logical_not(late))
    def _():
        permute.start()

    @pl.when(f == half)
    def _():
        by_turn(lambda turn: li_copy(half - 1, pl.ds(0, head_rows(turn))).start())

    @pl.when(f < n - 1)
    def _():
        pl.semaphore_wait(above.at[1], 1)

    @pl.when(f == half - 1)
    def _():
        by_turn(lambda turn: li_copy(half, pl.ds(0, head_rows(turn))).start())

    if n > 2:
        tell(above.at[2], f - 1, (f > 0) & (f + 1 < n))
        tell(below.at[2], f + 1, (f < n - 1) & (f - 1 >= 0))
    near(0)
    weights.start()
    own_li.start()
    ids[f] = jnp.full(ids.shape[1:], mid[0, 0], jnp.int32)

    def late_permute():
        pl.semaphore_wait(pair, 1)
        permute.start()

    pl.when(late & (f == 0))(late_permute)
    for d in range(2, n):
        @pl.when(f + d < n)
        def _():
            pl.semaphore_wait(above.at[d], 1)

        @pl.when(f - d >= 0)
        def _():
            pl.semaphore_wait(below.at[d], 1)

        if d + 1 < n:
            tell(above.at[d + 1], f - 1, (f > 0) & (f + d < n))
            tell(below.at[d + 1], f + 1, (f < n - 1) & (f - d >= 0))

    pl.when(late & (f > 0))(late_permute)
    permute.wait_recv()
    forward(0)
    near(1)
    for step in range(1, n):
        target = lax.rem(f + step, n)
        id_copy(target, f).start()
    def quota(step, turn):
        return min(total, step * (BETWEEN[turn]))

    def crossings(step, turn):
        for index in range(quota(step - 1, turn), quota(step, turn)):
            crossing(index, turn)

    for step in range(1, n - 1):
        by_turn(functools.partial(crossings, step))
        arrived(step)
        forward(step)
        near(step + 1)
    for piece in range(n, pieces):
        near(piece)

    def remaining(turn):
        begin = quota(n - 2, turn)
        middle = min(max(begin, INNER), total)
        for index in range(begin, middle):
            crossing(index, turn)
        inner()
        for index in range(middle, total):
            crossing(index, turn)

    by_turn(remaining)
    for distance in range(n - 1, 0, -1):
        @pl.when((f >= half) & (f + distance < n - 1))
        def _():
            li_copy(f + distance).start()

        @pl.when((f < half) & (f - distance > 0))
        def _():
            li_copy(f - distance).start()

    weights.wait()

    def input_block(block):
        gis[block] = lax.dot_general(
            inc[block], wv[...], (((1,), (1,)), ((), ())), preferred_element_type=jnp.float32
        ).astype(gis.dtype)

    arrived(n - 1)

    def input_blocks(block, carry):
        input_block(block)
        return carry

    lax.fori_loop(0, n, input_blocks, 0)

    @pl.when(at_once)
    def _():
        gi_send(n, f, gis, gi, gi_s, gi_r, own_s.at[2])

    own_li.wait()

    def others(action):
        def run(step, carry):
            action(lax.rem(f + step, n))
            return carry

        lax.fori_loop(1, n, run, 0)

    def li_wait(peer):
        pltpu.make_async_remote_copy(
            src_ref=share_of(li, peer, share),
            dst_ref=lix.at[peer],
            send_sem=li_s.at[peer],
            recv_sem=li_r.at[peer],
            device_id={"fsdp": peer},
            device_id_type=MESH,
        ).wait()
        id_copy(peer, peer).wait()

    others(li_wait)

    permute.wait_send()
    for step in range(n - 1):
        @pl.when((f - step >= 0) & (f < n - 1))
        def _():
            cot_copy(f - step, f + 1, right_s).wait_send()

        @pl.when((f + step < n) & (f > 0))
        def _():
            cot_copy(f + step, f - 1, left_s).wait_send()

    @pl.when(at_once)
    def _():
        gi_wait(n, f, gis, gi, gi_s, gi_r, own_s.at[2])


def weight_kernel(n, inc, lix, ids, gs_out, gq_out, token, gs, gq, sems):
    tokens, share = lix.shape[1:]
    columns = inc.shape[2]
    inverse = 1.0 / tokens
    exact = tokens & (tokens - 1) == 0
    tile = min(TILE, share)
    outs = ((gs, gs_out), (gq, gq_out))

    def out_copy(index, which):
        window = pl.ds(pl.multiple_of(index * tile, tile), tile)
        source, target = outs[which]
        return pltpu.make_async_copy(source.at[window], target.at[window], sems.at[which, index])

    def weight_rows(index, carry):
        start = pl.multiple_of(index * tile, tile)
        total, micro = None, [None] * MICRO
        for block in range(n):
            product = lax.dot_general(
                lix[block, :, pl.ds(start, tile)],
                inc[block],
                (((0,), (0,)), ((), ())),
                preferred_element_type=jnp.float32,
            )
            if not exact:
                product = product * inverse
            product = product.astype(jnp.bfloat16).astype(jnp.float32)
            total = product if total is None else total + product
            for m in range(1, MICRO):
                part = product * (ids[block][:1, :1] == m).astype(jnp.float32)
                micro[m] = part if micro[m] is None else micro[m] + part
        micro[0] = total
        for m in range(1, MICRO):
            micro[0] = micro[0] - micro[m]
        square = micro[0] * micro[0]
        for m in range(1, MICRO):
            square = square + micro[m] * micro[m]
        if exact:
            total, square = total * inverse, square * (inverse * inverse)
        gs[pl.ds(start, tile), :] = total
        gq[pl.ds(start, tile), :] = square
        for which in range(2):
            out_copy(index, which).start()
        return carry

    lax.fori_loop(0, share // tile, weight_rows, 0)
    token[...] = jnp.zeros_like(token)

    def finish(index, carry):
        for which in range(2):
            out_copy(index, which).wait()
        return carry

    lax.fori_loop(0, share // tile, finish, 0)


def late_kernel(n, gis, token, gi, gi_s, gi_r, own_s, above, below):
    f = lax.axis_index("fsdp")
    s = lax.axis_index("section")
    half = n // 2

    tokens = gis.shape[1]
    cut = tokens // 2

    def send(peer, cond, rows=slice(None)):
        @pl.when(cond)
        def _():
            gi_copy(peer, f, gis, gi, gi_s, gi_r, rows).start()

    @pl.when(lax.rem(s, 2) != AT_ONCE)
    def _():
        barrier = pltpu.get_barrier_semaphore()
        tell(barrier, f + 1, f < n - 1)

        @pl.when(f > 0)
        def _():
            pl.semaphore_wait(barrier, 1)

        tell(above.at[1], f - 1, f > 0)
        send(half - 1, f == half, pl.ds(0, cut))
        send(f - 1, (f > 0) & (f < half))

        @pl.when(f < n - 1)
        def _():
            pl.semaphore_wait(above.at[1], 1)

        send(half, f == half - 1, pl.ds(0, cut))
        if n > 2:
            tell(above.at[2], f - 1, (f > 0) & (f + 1 < n))
            tell(below.at[2], f + 1, (f < n - 1) & (f - 1 >= 0))
        send(f + 1, (f >= half) & (f < n - 1))
        for d in range(2, n):
            @pl.when(f + d < n)
            def _():
                pl.semaphore_wait(above.at[d], 1)

            @pl.when(f - d >= 0)
            def _():
                pl.semaphore_wait(below.at[d], 1)

            if d + 1 < n:
                tell(above.at[d + 1], f - 1, (f > 0) & (f + d < n))
                tell(below.at[d + 1], f + 1, (f < n - 1) & (f - d >= 0))
        for d in range(n - 1, 1, -1):
            send(f + d, (f + d < n) & ((f >= half) | (f + d > half)))
            send(f - d, (f - d >= 0) & ((f < half) | (f - d < half - 1)))
        for d in range(n - 1, 0, -1):
            send(f + d, f + d < half)
            send(f - d, f - d >= half)
        send(half - 1, f == half, pl.ds(cut, tokens - cut))
        send(half, f == half - 1, pl.ds(cut, tokens - cut))
        send(half, f < half - 1)
        send(half - 1, f > half)
        pltpu.make_async_copy(gis.at[f], share_of(gi, f, gis.shape[2]), own_s).start()
        gi_wait(n, f, gis, gi, gi_s, gi_r, own_s)


def settle_kernel(early, late, out, sem):
    s = lax.axis_index("section")
    at_once = lax.rem(s, 2) == AT_ONCE

    @pl.when(at_once)
    def _():
        copy = pltpu.make_async_copy(early, out, sem)
        copy.start()
        copy.wait()

    @pl.when(jnp.logical_not(at_once))
    def _():
        copy = pltpu.make_async_copy(late, out, sem)
        copy.start()
        copy.wait()


def body(layer_input, next_cot, w_value, micro_ids):
    n = lax.axis_size("fsdp")
    ns = lax.axis_size("section")
    tokens, width = layer_input.shape[1:]
    share, columns = w_value.shape[1:]
    hbm, vmem = pl.BlockSpec(memory_space=pltpu.HBM), pl.BlockSpec(memory_space=pltpu.VMEM)
    anywhere = pl.BlockSpec(memory_space=pl.ANY)
    dma, regular = pltpu.SemaphoreType.DMA, pltpu.SemaphoreType.REGULAR
    shape = jax.ShapeDtypeStruct
    stay = functools.partial(pltpu.with_memory_space_constraint, memory_space=pltpu.HBM)
    near = functools.partial(pltpu.with_memory_space_constraint, memory_space=pltpu.VMEM)
    early, gis, inc, lix, ids = pl.pallas_call(
        functools.partial(kernel, n, ns),
        out_shape=(
            shape((tokens, width), jnp.bfloat16),
            shape((n, tokens, share), jnp.bfloat16),
            shape((n, tokens, columns), jnp.bfloat16),
            shape((n, tokens, share), jnp.bfloat16),
            shape((n, 8, 128), jnp.int32),
        ),
        in_specs=[hbm, hbm, hbm, pl.BlockSpec(memory_space=pltpu.SMEM)],
        out_specs=(anywhere, vmem, vmem, vmem, vmem),
        scratch_shapes=[
            pltpu.VMEM((share, columns), jnp.bfloat16),
            dma, dma, dma((n,)), dma((n,)), dma((n,)), dma((n,)), dma((n,)),
            dma((n,)), dma((n,)), dma((n,)), dma((n,)), dma((3,)),
            regular((n,)), regular((n,)), regular,
        ],
        compiler_params=pltpu.CompilerParams(
            collective_id=0, has_side_effects=True, vmem_limit_bytes=40 * 2**20
        ),
    )(stay(layer_input[0]), stay(next_cot[0]), stay(w_value[0]), micro_ids)
    wide = shape((share, columns), jnp.float32)
    grad_sum, grad_square, token = pl.pallas_call(
        functools.partial(weight_kernel, n),
        out_shape=(wide, wide, shape((8, 128), jnp.float32)),
        in_specs=[vmem, vmem, vmem],
        out_specs=(hbm, hbm, vmem),
        scratch_shapes=[
            pltpu.VMEM((share, columns), jnp.float32),
            pltpu.VMEM((share, columns), jnp.float32),
            dma((2, share // min(TILE, share))),
        ],
        compiler_params=pltpu.CompilerParams(vmem_limit_bytes=16 * 2**20),
    )(inc, lix, ids)
    late = pl.pallas_call(
        functools.partial(late_kernel, n),
        out_shape=shape((tokens, width), jnp.bfloat16),
        in_specs=[vmem, anywhere],
        out_specs=anywhere,
        scratch_shapes=[dma((n,)), dma((n,)), dma, regular((n,)), regular((n,))],
        compiler_params=pltpu.CompilerParams(
            collective_id=1, has_side_effects=True, vmem_limit_bytes=40 * 2**20
        ),
    )(gis, token)
    grad_input = pl.pallas_call(
        settle_kernel,
        out_shape=shape((tokens, width), jnp.bfloat16),
        in_specs=[anywhere, anywhere],
        out_specs=hbm,
        scratch_shapes=[dma],
        compiler_params=pltpu.CompilerParams(vmem_limit_bytes=4 * 2**20),
    )(near(early), near(late))
    return (grad_input[None], grad_sum[None], grad_square[None])


def solution(mesh):
    spec = P("section", "fsdp", None)
    return jax.shard_map(
        body,
        mesh=mesh,
        in_specs=(spec, spec, spec, P("section", "fsdp")),
        out_specs=(spec, spec, spec),
        check_vma=False,
    )
```

time: 58.7 us -> 58.4 us (level)
  the two profiles are of different devices: /device:TPU:13 before, /device:TPU:10 now
where the time goes in v3:
time: 58.4 us; the launch traced here: 58.2 us
  Pallas kernels  56.9 us (97%)
  between operations  1.3 us (2%)
    pallas_call x1, Pallas kernels, body(): pl.pallas_call(functools.partial(kernel, n, ns), out_shape=(shape((tokens...  33.8 us
    pallas_call x1, Pallas kernels, body(): pl.pallas_call(functools.partial(late_kernel, n), out_shape=shape((tokens...  18.4 us
    pallas_call x1, Pallas kernels, body(): pl.pallas_call(functools.partial(weight_kernel, n), out_shape=(wide, wide...  3.75 us

profile of v3, /device:TPU:10, one launch (start us, length us, event | category | flops | bytes accessed | tf_op | source)
XLA Modules:
  0.0 58.2 jit_solution(10534371795661924090)
XLA Ops:
  1.3 33.8 %shard_map.67 = (bf16[128,4096]{1,0:T(8,128)(2,1)S(1)}, bf16[4,128,1024]{2,1,0:T(8,128)(2,1)S(1)}, bf16[4,128,512]{2,1,0:T(8,128)(2,1)S(1)}, bf16[4,128,1024]{2,1,0:T(8,128)(2,1)S(1)}, s32[4,8,128]{2,1,0:T(8,128)S(1)}) custom-call(bf16[128,4096]{1,0:T(8,128)(2,1)} %bitcast.7, bf16[128,512]{1,0:T(8,128)(2,1)} %bitcast.9, bf16[1024,512]{1,0:T(8,128)(2,1)} %bitcast.8, ...), custom_call_target="tpu_custom_call" | custom-call | tf_op jit(solution)/shard_map/pallas_call | solution.py:500
  35.1 3.8 %shard_map.68 = (f32[1024,512]{1,0:T(8,128)}, f32[1024,512]{1,0:T(8,128)}, f32[8,128]{1,0:T(8,128)S(1)}) custom-call(bf16[4,128,512]{2,1,0:T(8,128)(2,1)S(1)} %get-tuple-element.13.inc, bf16[4,128,1024]{2,1,0:T(8,128)(2,1)S(1)} %get-tuple-element.14.lix, s32[4,8,128]{2,1,0:T(8,128)S(1)} %get-tuple-element.15.ids), custom_call_target="tpu_custom_call" | custom-call | tf_op jit(solution)/shard_map/pallas_call | solution.py:522
  38.8 18.4 %shard_map.69.late = bf16[128,4096]{1,0:T(8,128)(2,1)S(1)} custom-call(bf16[4,128,1024]{2,1,0:T(8,128)(2,1)S(1)} %get-tuple-element.12.gis, f32[8,128]{1,0:T(8,128)S(1)} %get-tuple-element.16.token), custom_call_target="tpu_custom_call" | custom-call | tf_op jit(solution)/shard_map/pallas_call | solution.py:534
  57.2 1.0 %shard_map.70 = bf16[128,4096]{1,0:T(8,128)(2,1)} custom-call(bf16[128,4096]{1,0:T(8,128)(2,1)S(1)} %get-tuple-element.11.early, bf16[128,4096]{1,0:T(8,128)(2,1)S(1)} %shard_map.69.late), custom_call_target="tpu_custom_call" | custom-call | tf_op jit(solution)/shard_map/pallas_call | solution.py:544

commit v4 on v3

--- a/solution.py
+++ b/solution.py
@@ -10,10 +10,10 @@
 MICRO = 2
 MESH = pl.DeviceIdType.MESH
 PIECES = 4
-HEAD = (3, 2, 2, 3)
-BETWEEN = (2, 1, 2, 2)
+HEAD = 3
+BETWEEN = (1, 2)
 TILE = 256
-AT_ONCE = 1
+AT_ONCE = 0
 INNER = 4
 
 
@@ -72,13 +72,6 @@
     behind = lax.rem(s + ns - 1, ns)
     ahead = lax.rem(s + 1, ns)
     at_once = lax.rem(s, 2) == AT_ONCE
-    early_ahead = lax.rem(ahead, 4) != 0
-    turns = (
-        jnp.logical_not(at_once),
-        at_once & early_ahead,
-        at_once & jnp.logical_not(early_ahead) & (s < ns - 1),
-        at_once & jnp.logical_not(early_ahead) & (s == ns - 1),
-    )
     tokens, share = lix.shape[1], lix.shape[2]
     columns = inc.shape[2]
 
@@ -123,7 +116,7 @@
     weights = pltpu.make_async_copy(w, wv, own_s.at[0])
     own_li = pltpu.make_async_copy(share_of(li, f, share), lix.at[f], own_s.at[1])
 
-    late, late_ahead = lax.rem(s, 4) == 0, lax.rem(ahead, 4) == 0
+    late, late_ahead = s == 0, ahead == 0
     barrier = pltpu.get_barrier_semaphore()
     tell(barrier, f + 1, f < n - 1)
 
@@ -151,17 +144,12 @@
     half = n // 2
     total = half * pieces
 
-    def head_rows(turn):
-        return min(HEAD[turn], pieces) * rows
-
-    def by_turn(action):
-        for turn, condition in enumerate(turns):
-            pl.when(condition)(functools.partial(action, turn))
-
-    def crossing(index, turn):
+    head = min(HEAD, pieces)
+
+    def crossing(index):
         owner, piece = index // pieces, index % pieces
         window = pl.ds(piece * rows, rows)
-        done = owner == half - 1 and piece * rows < head_rows(turn)
+        done = owner == half - 1 and piece < head
 
         @pl.when((f < half - 1) if done else (f < half))
         def _():
@@ -220,7 +208,7 @@
 
     @pl.when(f == half)
     def _():
-        by_turn(lambda turn: li_copy(half - 1, pl.ds(0, head_rows(turn))).start())
+        li_copy(half - 1, pl.ds(0, head * rows)).start()
 
     @pl.when(f < n - 1)
     def _():
@@ -228,7 +216,7 @@
 
     @pl.when(f == half - 1)
     def _():
-        by_turn(lambda turn: li_copy(half, pl.ds(0, head_rows(turn))).start())
+        li_copy(half, pl.ds(0, head * rows)).start()
 
     if n > 2:
         tell(above.at[2], f - 1, (f > 0) & (f + 1 < n))
@@ -263,31 +251,35 @@
     for step in range(1, n):
         target = lax.rem(f + step, n)
         id_copy(target, f).start()
-    def quota(step, turn):
-        return min(total, step * (BETWEEN[turn]))
-
-    def crossings(step, turn):
-        for index in range(quota(step - 1, turn), quota(step, turn)):
-            crossing(index, turn)
+    def by_section(action):
+        for which, condition in enumerate((s < ns - 1, s == ns - 1)):
+            pl.when(condition)(functools.partial(action, which))
+
+    def quota(step, which):
+        return min(total, step * BETWEEN[which])
+
+    def crossings(step, which):
+        for index in range(quota(step - 1, which), quota(step, which)):
+            crossing(index)
 
     for step in range(1, n - 1):
-        by_turn(functools.partial(crossings, step))
+        by_section(functools.partial(crossings, step))
         arrived(step)
         forward(step)
         near(step + 1)
     for piece in range(n, pieces):
         near(piece)
 
-    def remaining(turn):
-        begin = quota(n - 2, turn)
+    def remaining(which):
+        begin = quota(n - 2, which)
         middle = min(max(begin, INNER), total)
         for index in range(begin, middle):
-            crossing(index, turn)
+            crossing(index)
         inner()
         for index in range(middle, total):
-            crossing(index, turn)
-
-    by_turn(remaining)
+            crossing(index)
+
+    by_section(remaining)
     for distance in range(n - 1, 0, -1):
         @pl.when((f >= half) & (f + distance < n - 1))
         def _():
@@ -433,6 +425,7 @@
         tell(above.at[1], f - 1, f > 0)
         send(half - 1, f == half, pl.ds(0, cut))
         send(f - 1, (f > 0) & (f < half))
+        send(f - 1, f > half, pl.ds(0, cut))
 
         @pl.when(f < n - 1)
         def _():
@@ -443,6 +436,7 @@
             tell(above.at[2], f - 1, (f > 0) & (f + 1 < n))
             tell(below.at[2], f + 1, (f < n - 1) & (f - 1 >= 0))
         send(f + 1, (f >= half) & (f < n - 1))
+        send(f + 1, f + 1 < half, pl.ds(0, cut))
         for d in range(2, n):
             @pl.when(f + d < n)
             def _():
@@ -456,15 +450,14 @@
                 tell(above.at[d + 1], f - 1, (f > 0) & (f + d < n))
                 tell(below.at[d + 1], f + 1, (f < n - 1) & (f - d >= 0))
         for d in range(n - 1, 1, -1):
-            send(f + d, (f + d < n) & ((f >= half) | (f + d > half)))
-            send(f - d, (f - d >= 0) & ((f < half) | (f - d < half - 1)))
-        for d in range(n - 1, 0, -1):
-            send(f + d, f + d < half)
-            send(f - d, f - d >= half)
+            send(f + d, (f + d < n) & ((f >= half) | (f + d != half)))
+            send(f - d, (f - d >= 0) & ((f < half) | (f - d != half - 1)))
+        send(f - 1, f > half, pl.ds(cut, tokens - cut))
+        send(f + 1, f + 1 < half, pl.ds(cut, tokens - cut))
+        send(half, f < half - 1)
+        send(half - 1, f > half)
         send(half - 1, f == half, pl.ds(cut, tokens - cut))
         send(half, f == half - 1, pl.ds(cut, tokens - cut))
-        send(half, f < half - 1)
-        send(half - 1, f > half)
         pltpu.make_async_copy(gis.at[f], share_of(gi, f, gis.shape[2]), own_s).start()
         gi_wait(n, f, gis, gi, gi_s, gi_r, own_s)
 

time: 58.4 us -> 57.4 us (0.983)
  the two profiles are of different devices: /device:TPU:10 before, /device:TPU:13 now
where the time goes in v4:
time: 57.4 us; the launch traced here: 57.2 us
  Pallas kernels  55.9 us (97%)
  between operations  1.3 us (2%)
    pallas_call x1, Pallas kernels, body(): pl.pallas_call(functools.partial(kernel, n, ns), out_shape=(shape((tokens...  33 us
    pallas_call x1, Pallas kernels, body(): pl.pallas_call(functools.partial(late_kernel, n), out_shape=shape((tokens...  18.1 us
    pallas_call x1, Pallas kernels, body(): pl.pallas_call(functools.partial(weight_kernel, n), out_shape=(wide, wide...  3.75 us

profile of v4, /device:TPU:13, one launch (start us, length us, event | category | flops | bytes accessed | tf_op | source)
XLA Modules:
  0.0 57.2 jit_solution(16622336136268658343)
XLA Ops:
  1.3 33.0 %shard_map.67 = (bf16[128,4096]{1,0:T(8,128)(2,1)S(1)}, bf16[4,128,1024]{2,1,0:T(8,128)(2,1)S(1)}, bf16[4,128,512]{2,1,0:T(8,128)(2,1)S(1)}, bf16[4,128,1024]{2,1,0:T(8,128)(2,1)S(1)}, s32[4,8,128]{2,1,0:T(8,128)S(1)}) custom-call(bf16[128,4096]{1,0:T(8,128)(2,1)} %bitcast.7, bf16[128,512]{1,0:T(8,128)(2,1)} %bitcast.9, bf16[1024,512]{1,0:T(8,128)(2,1)} %bitcast.8, ...), custom_call_target="tpu_custom_call" | custom-call | tf_op jit(solution)/shard_map/pallas_call | solution.py:493
  34.3 3.8 %shard_map.68 = (f32[1024,512]{1,0:T(8,128)}, f32[1024,512]{1,0:T(8,128)}, f32[8,128]{1,0:T(8,128)S(1)}) custom-call(bf16[4,128,512]{2,1,0:T(8,128)(2,1)S(1)} %get-tuple-element.13.inc, bf16[4,128,1024]{2,1,0:T(8,128)(2,1)S(1)} %get-tuple-element.14.lix, s32[4,8,128]{2,1,0:T(8,128)S(1)} %get-tuple-element.15.ids), custom_call_target="tpu_custom_call" | custom-call | tf_op jit(solution)/shard_map/pallas_call | solution.py:515
  38.1 18.1 %shard_map.69.late = bf16[128,4096]{1,0:T(8,128)(2,1)S(1)} custom-call(bf16[4,128,1024]{2,1,0:T(8,128)(2,1)S(1)} %get-tuple-element.12.gis, f32[8,128]{1,0:T(8,128)S(1)} %get-tuple-element.16.token), custom_call_target="tpu_custom_call" | custom-call | tf_op jit(solution)/shard_map/pallas_call | solution.py:527
  56.2 1.0 %shard_map.70 = bf16[128,4096]{1,0:T(8,128)(2,1)} custom-call(bf16[128,4096]{1,0:T(8,128)(2,1)S(1)} %get-tuple-element.11.early, bf16[128,4096]{1,0:T(8,128)(2,1)S(1)} %shard_map.69.late), custom_call_target="tpu_custom_call" | custom-call | tf_op jit(solution)/shard_map/pallas_call | solution.py:537

commit v5 on v4

--- a/solution.py
+++ b/solution.py
@@ -465,18 +465,21 @@
 def settle_kernel(early, late, out, sem):
     s = lax.axis_index("section")
     at_once = lax.rem(s, 2) == AT_ONCE
-
-    @pl.when(at_once)
-    def _():
-        copy = pltpu.make_async_copy(early, out, sem)
-        copy.start()
-        copy.wait()
-
-    @pl.when(jnp.logical_not(at_once))
-    def _():
-        copy = pltpu.make_async_copy(late, out, sem)
-        copy.start()
-        copy.wait()
+    parts = sem.shape[0]
+    rows = out.shape[0] // parts
+
+    def settle(source):
+        copies = [
+            pltpu.make_async_copy(source.at[pl.ds(p * rows, rows)], out.at[pl.ds(p * rows, rows)], sem.at[p])
+            for p in range(parts)
+        ]
+        for copy in copies:
+            copy.start()
+        for copy in copies:
+            copy.wait()
+
+    pl.when(at_once)(functools.partial(settle, early))
+    pl.when(jnp.logical_not(at_once))(functools.partial(settle, late))
 
 
 def body(layer_input, next_cot, w_value, micro_ids):
@@ -539,7 +542,7 @@
         out_shape=shape((tokens, width), jnp.bfloat16),
         in_specs=[anywhere, anywhere],
         out_specs=hbm,
-        scratch_shapes=[dma],
+        scratch_shapes=[dma((4,))],
         compiler_params=pltpu.CompilerParams(vmem_limit_bytes=4 * 2**20),
     )(near(early), near(late))
     return (grad_input[None], grad_sum[None], grad_square[None])

time: 57.4 us -> 57.4 us (level)
  no operation moved by 1% of the time
where the time goes in v5:
time: 57.4 us; the launch traced here: 57.2 us
  Pallas kernels  55.9 us (97%)
  between operations  1.3 us (2%)
    pallas_call x1, Pallas kernels, body(): pl.pallas_call(functools.partial(kernel, n, ns), out_shape=(shape((tokens...  33 us
    pallas_call x1, Pallas kernels, body(): pl.pallas_call(functools.partial(late_kernel, n), out_shape=shape((tokens...  18.1 us
    pallas_call x1, Pallas kernels, body(): pl.pallas_call(functools.partial(weight_kernel, n), out_shape=(wide, wide...  3.75 us

profile of v5, /device:TPU:13, one launch (start us, length us, event | category | flops | bytes accessed | tf_op | source)
XLA Modules:
  0.0 57.2 jit_solution(13879437752872141538)
XLA Ops:
  1.3 33.0 %shard_map.67 = (bf16[128,4096]{1,0:T(8,128)(2,1)S(1)}, bf16[4,128,1024]{2,1,0:T(8,128)(2,1)S(1)}, bf16[4,128,512]{2,1,0:T(8,128)(2,1)S(1)}, bf16[4,128,1024]{2,1,0:T(8,128)(2,1)S(1)}, s32[4,8,128]{2,1,0:T(8,128)S(1)}) custom-call(bf16[128,4096]{1,0:T(8,128)(2,1)} %bitcast.7, bf16[128,512]{1,0:T(8,128)(2,1)} %bitcast.9, bf16[1024,512]{1,0:T(8,128)(2,1)} %bitcast.8, ...), custom_call_target="tpu_custom_call" | custom-call | tf_op jit(solution)/shard_map/pallas_call | solution.py:496
  34.3 3.8 %shard_map.68 = (f32[1024,512]{1,0:T(8,128)}, f32[1024,512]{1,0:T(8,128)}, f32[8,128]{1,0:T(8,128)S(1)}) custom-call(bf16[4,128,512]{2,1,0:T(8,128)(2,1)S(1)} %get-tuple-element.13.inc, bf16[4,128,1024]{2,1,0:T(8,128)(2,1)S(1)} %get-tuple-element.14.lix, s32[4,8,128]{2,1,0:T(8,128)S(1)} %get-tuple-element.15.ids), custom_call_target="tpu_custom_call" | custom-call | tf_op jit(solution)/shard_map/pallas_call | solution.py:518
  38.1 18.1 %shard_map.69.late = bf16[128,4096]{1,0:T(8,128)(2,1)S(1)} custom-call(bf16[4,128,1024]{2,1,0:T(8,128)(2,1)S(1)} %get-tuple-element.12.gis, f32[8,128]{1,0:T(8,128)S(1)} %get-tuple-element.16.token), custom_call_target="tpu_custom_call" | custom-call | tf_op jit(solution)/shard_map/pallas_call | solution.py:530
  56.2 1.0 %shard_map.70 = bf16[128,4096]{1,0:T(8,128)(2,1)} custom-call(bf16[128,4096]{1,0:T(8,128)(2,1)S(1)} %get-tuple-element.11.early, bf16[128,4096]{1,0:T(8,128)(2,1)S(1)} %shard_map.69.late), custom_call_target="tpu_custom_call" | custom-call | tf_op jit(solution)/shard_map/pallas_call | solution.py:540

commit v6 on v4

--- a/solution.py
+++ b/solution.py
@@ -65,7 +65,7 @@
 def kernel(
     n, ns, li, cot, w, mid, gi, gis, inc, lix, ids, wv,
     perm_s, perm_r, right_s, left_s, cot_r, li_s, li_r, gi_s, gi_r, id_s, id_r, own_s,
-    above, below, pair,
+    above, below, pair, ready,
 ):
     f = lax.axis_index("fsdp")
     s = lax.axis_index("section")
@@ -116,6 +116,35 @@
     weights = pltpu.make_async_copy(w, wv, own_s.at[0])
     own_li = pltpu.make_async_copy(share_of(li, f, share), lix.at[f], own_s.at[1])
 
+    pieces = PIECES
+    rows = tokens // pieces
+    half = n // 2
+    total = half * pieces
+    head = min(HEAD, pieces)
+    opposite = 2 * half - 1 - f
+    first_window = pl.ds(0, head * rows)
+    staged = ((f == half - 1) | (f == half)) & (s < ns - 2)
+
+    first_rows = pltpu.make_async_copy(share_of(li, opposite, share, first_window), ready, own_s.at[3])
+    pl.when(staged)(first_rows.start)
+
+    def send_first_rows():
+        @pl.when(staged)
+        def _():
+            first_rows.wait()
+            pltpu.make_async_remote_copy(
+                src_ref=ready,
+                dst_ref=lix.at[f, first_window],
+                send_sem=li_s.at[opposite],
+                recv_sem=li_r.at[f],
+                device_id={"fsdp": opposite},
+                device_id_type=MESH,
+            ).start()
+
+        @pl.when(jnp.logical_not(staged))
+        def _():
+            li_copy(opposite, first_window).start()
+
     late, late_ahead = s == 0, ahead == 0
     barrier = pltpu.get_barrier_semaphore()
     tell(barrier, f + 1, f < n - 1)
@@ -137,14 +166,6 @@
     @pl.when(late_ahead)
     def _():
         pl.semaphore_signal(pair, inc=1, device_id={"section": ahead}, device_id_type=MESH)
-
-    pieces = PIECES
-    rows = tokens // pieces
-
-    half = n // 2
-    total = half * pieces
-
-    head = min(HEAD, pieces)
 
     def crossing(index):
         owner, piece = index // pieces, index % pieces
@@ -208,7 +229,7 @@
 
     @pl.when(f == half)
     def _():
-        li_copy(half - 1, pl.ds(0, head * rows)).start()
+        send_first_rows()
 
     @pl.when(f < n - 1)
     def _():
@@ -216,7 +237,7 @@
 
     @pl.when(f == half - 1)
     def _():
-        li_copy(half, pl.ds(0, head * rows)).start()
+        send_first_rows()
 
     if n > 2:
         tell(above.at[2], f - 1, (f > 0) & (f + 1 < n))
@@ -504,8 +525,9 @@
         scratch_shapes=[
             pltpu.VMEM((share, columns), jnp.bfloat16),
             dma, dma, dma((n,)), dma((n,)), dma((n,)), dma((n,)), dma((n,)),
-            dma((n,)), dma((n,)), dma((n,)), dma((n,)), dma((3,)),
+            dma((n,)), dma((n,)), dma((n,)), dma((n,)), dma((4,)),
             regular((n,)), regular((n,)), regular,
+            pltpu.VMEM((min(HEAD, PIECES) * (tokens // PIECES), share), jnp.bfloat16),
         ],
         compiler_params=pltpu.CompilerParams(
             collective_id=0, has_side_effects=True, vmem_limit_bytes=40 * 2**20

time: 57.4 us -> 57.3 us (level)
    pallas_call x1, Pallas kernels: 33 us -> 31.7 us  [body(): pl.pallas_call(functools.partial(kernel, n, ns), out_shape=(shape((tokens...]
    pallas_call x1, Pallas kernels: 18.1 us -> 19.3 us  [body(): pl.pallas_call(functools.partial(late_kernel, n), out_shape=shape((tokens...]
where the time goes in v6:
time: 57.3 us; the launch traced here: 57 us
  Pallas kernels  55.7 us (97%)
  between operations  1.3 us (2%)
    pallas_call x1, Pallas kernels, body(): pl.pallas_call(functools.partial(kernel, n, ns), out_shape=(shape((tokens...  31.7 us
    pallas_call x1, Pallas kernels, body(): pl.pallas_call(functools.partial(late_kernel, n), out_shape=shape((tokens...  19.3 us
    pallas_call x1, Pallas kernels, body(): pl.pallas_call(functools.partial(weight_kernel, n), out_shape=(wide, wide...  3.75 us

profile of v6, /device:TPU:13, one launch (start us, length us, event | category | flops | bytes accessed | tf_op | source)
XLA Modules:
  0.0 57.0 jit_solution(2818815215372414012)
XLA Ops:
  1.3 31.7 %shard_map.67 = (bf16[128,4096]{1,0:T(8,128)(2,1)S(1)}, bf16[4,128,1024]{2,1,0:T(8,128)(2,1)S(1)}, bf16[4,128,512]{2,1,0:T(8,128)(2,1)S(1)}, bf16[4,128,1024]{2,1,0:T(8,128)(2,1)S(1)}, s32[4,8,128]{2,1,0:T(8,128)S(1)}) custom-call(bf16[128,4096]{1,0:T(8,128)(2,1)} %bitcast.7, bf16[128,512]{1,0:T(8,128)(2,1)} %bitcast.9, bf16[1024,512]{1,0:T(8,128)(2,1)} %bitcast.8, ...), custom_call_target="tpu_custom_call" | custom-call | tf_op jit(solution)/shard_map/pallas_call | solution.py:514
  33.0 3.8 %shard_map.68 = (f32[1024,512]{1,0:T(8,128)}, f32[1024,512]{1,0:T(8,128)}, f32[8,128]{1,0:T(8,128)S(1)}) custom-call(bf16[4,128,512]{2,1,0:T(8,128)(2,1)S(1)} %get-tuple-element.13.inc, bf16[4,128,1024]{2,1,0:T(8,128)(2,1)S(1)} %get-tuple-element.14.lix, s32[4,8,128]{2,1,0:T(8,128)S(1)} %get-tuple-element.15.ids), custom_call_target="tpu_custom_call" | custom-call | tf_op jit(solution)/shard_map/pallas_call | solution.py:537
  36.8 19.3 %shard_map.69.late = bf16[128,4096]{1,0:T(8,128)(2,1)S(1)} custom-call(bf16[4,128,1024]{2,1,0:T(8,128)(2,1)S(1)} %get-tuple-element.12.gis, f32[8,128]{1,0:T(8,128)S(1)} %get-tuple-element.16.token), custom_call_target="tpu_custom_call" | custom-call | tf_op jit(solution)/shard_map/pallas_call | solution.py:549
  56.0 1.0 %shard_map.70 = bf16[128,4096]{1,0:T(8,128)(2,1)} custom-call(bf16[128,4096]{1,0:T(8,128)(2,1)S(1)} %get-tuple-element.11.early, bf16[128,4096]{1,0:T(8,128)(2,1)S(1)} %shard_map.69.late), custom_call_target="tpu_custom_call" | custom-call | tf_op jit(solution)/shard_map/pallas_call | solution.py:559
